TPU v7x, 32 devices: a whole 2x2x4 slice. The times are simulated.
32 devices in a mesh: batch: 8 (over z, y), fsdp: 4 (over x, core).
Axes of the slice: x: 2, y: 2, z: 4, core: 2. Of those that a mesh axis runs over, the one named last changes fastest.
Arguments:
- tokens: bfloat16 [128, 256, 768], P(('batch', 'fsdp')), may hold values from -6 to 6
- cotangent: bfloat16 [128, 256, 768], P(('batch', 'fsdp')), may hold values from -6 to 6
- mask_pos: int32 [128, 128], P(('batch', 'fsdp')), may hold values from 0 to 255, as said below
- mask_count: int32 [128], P(('batch', 'fsdp')), may hold values from 8 to 128, as said below
- w_qkv: float32 [768, 2304], P('fsdp'), may hold values from -0.21875 to 0.21875
- m_qkv: float32 [768, 2304], P(('fsdp', 'batch')), may hold values from -217.2232 to 217.2232
- v_qkv: float32 [768, 2304], P(('fsdp', 'batch')), may hold values from 1474.56 to 23592.96
- w_out: float32 [768, 768], P('fsdp'), may hold values from -0.875 to 0.875
- m_out: float32 [768, 768], P(('fsdp', 'batch')), may hold values from -50.685413 to 50.685413
- v_out: float32 [768, 768], P(('fsdp', 'batch')), may hold values from 80.2816 to 1284.5056
- w_fc1: float32 [768, 3072], P('fsdp'), may hold values from -0.21875 to 0.21875
- m_fc1: float32 [768, 3072], P(('fsdp', 'batch')), may hold values from -86.88928 to 86.88928
- v_fc1: float32 [768, 3072], P(('fsdp', 'batch')), may hold values from 235.9296 to 3774.8735
- w_fc2: float32 [3072, 768], P('fsdp'), may hold values from -0.109375 to 0.109375
- m_fc2: float32 [3072, 768], P(('fsdp', 'batch')), may hold values from -181.01933 to 181.01933
- v_fc2: float32 [3072, 768], P(('fsdp', 'batch')), may hold values from 1024 to 16384
- vectors: float32 [14, 768], P(None, 'fsdp'), may hold values from -1.2 to 1.6
- m_vec: float32 [14, 768], P(None, ('fsdp', 'batch')), may hold values from -217.2232 to 217.2232
- v_vec: float32 [14, 768], P(None, ('fsdp', 'batch')), may hold values from 1474.56 to 23592.96
Outputs:
- layer_out: bfloat16 [128, 256, 768], P(('batch', 'fsdp'))
- grad_tokens: float32 [128, 256, 768], P(('batch', 'fsdp'))
- new_w_qkv: float32 [768, 2304], P('fsdp')
- new_m_qkv: float32 [768, 2304], P(('fsdp', 'batch'))
- new_v_qkv: float32 [768, 2304], P(('fsdp', 'batch'))
- new_w_out: float32 [768, 768], P('fsdp')
- new_m_out: float32 [768, 768], P(('fsdp', 'batch'))
- new_v_out: float32 [768, 768], P(('fsdp', 'batch'))
- new_w_fc1: float32 [768, 3072], P('fsdp')
- new_m_fc1: float32 [768, 3072], P(('fsdp', 'batch'))
- new_v_fc1: float32 [768, 3072], P(('fsdp', 'batch'))
- new_w_fc2: float32 [3072, 768], P('fsdp')
- new_m_fc2: float32 [3072, 768], P(('fsdp', 'batch'))
- new_v_fc2: float32 [3072, 768], P(('fsdp', 'batch'))
- new_vectors: float32 [14, 768], P(None, 'fsdp')
- new_m_vec: float32 [14, 768], P(None, ('fsdp', 'batch'))
- new_v_vec: float32 [14, 768], P(None, ('fsdp', 'batch'))
Inputs may be any that keep to these rules, and one draw needn't show every extreme that they name: `mask_pos`: each row holds 128 different positions of the pair; its first mask_count entries are the masked tokens. `mask_count`: some pair has 128 masked tokens.
All inputs are finite; a program needn't handle non-finite values.
Results may differ from a plain program's by a relative error of at most 0.015.
Values may be sent and summed in bfloat16 or wider, within the bound.
No kernel may reach another device: no remote copies, remote signals or barrier semaphores. Data moves between devices by JAX's collectives and lax.ppermute only.
A program may use at most 192 MiB of HBM per device.

v0:
```python
import math
import jax
import jax.numpy as jnp
from jax import lax
from jax.sharding import PartitionSpec as P

D = 768
HEADS = 12
HDIM = 64
FF = 3072
TEXT = 40
STEP = 3
MAXM = 128
BETA_ONE = 0.5
BETA_TWO = 0.5
EPS_ADAM = 1e-08
STEP_RATES = (0.03, 0.1, 0.03, 0.015, 0.3)
DECAY_RATES = (0.01, 0.01, 0.01, 0.01, 0.0)
INV_ROOT_TWO = 1.0 / math.sqrt(2.0)
INV_ROOT_TWOPI = 1.0 / math.sqrt(2.0 * math.pi)


def dot_first(left_mat, right_mat):
    return lax.dot_general(
        left_mat, right_mat, (((0,), (0,)), ((), ())), preferred_element_type=jnp.float32
    )


def dot_last(left_mat, right_mat):
    return lax.dot_general(
        left_mat, right_mat, (((1,), (1,)), ((), ())), preferred_element_type=jnp.float32
    )


def normalize(hidden):
    row_mean = jnp.mean(hidden, axis=-1, keepdims=True)
    centred = hidden - row_mean
    inv_scale = lax.rsqrt(jnp.mean(centred * centred, axis=-1, keepdims=True) + 1e-06)
    return (centred * inv_scale, inv_scale)


def norm_back(gradient, normed, inv_scale, gain_row):
    scaled = gradient * gain_row
    return inv_scale * (
        scaled
        - jnp.mean(scaled, axis=-1, keepdims=True)
        - normed * jnp.mean(scaled * normed, axis=-1, keepdims=True)
    )


def adamw(weight, gradient, moment_one, moment_two, step_rate, decay_rate):
    new_first = BETA_ONE * moment_one + (1.0 - BETA_ONE) * gradient
    new_second = BETA_TWO * moment_two + (1.0 - BETA_TWO) * gradient * gradient
    correct_one = 1.0 - BETA_ONE**STEP
    correct_two = 1.0 - BETA_TWO**STEP
    update = (
        new_first / correct_one / (jnp.sqrt(new_second / correct_two) + EPS_ADAM)
        + decay_rate * weight
    )
    return (weight - step_rate * update, new_first, new_second)


def shards(
    tokens,
    cotangent,
    mask_pos,
    mask_count,
    w_qkv,
    m_qkv,
    v_qkv,
    w_out,
    m_out,
    v_out,
    w_fc1,
    m_fc1,
    v_fc1,
    w_fc2,
    m_fc2,
    v_fc2,
    vectors,
    m_vec,
    v_vec,
):
    pair_count, length, model_width = tokens.shape
    token_rows = pair_count * length
    fc1_parts = FF // D
    attn_scale = HDIM ** (-0.5)
    shard_qkv = w_qkv.astype(jnp.bfloat16)
    shard_out = w_out.astype(jnp.bfloat16)
    shard_fc1 = w_fc1.astype(jnp.bfloat16)
    shard_fc2 = w_fc2.astype(jnp.bfloat16)
    shard_vec = vectors.astype(jnp.bfloat16)
    qkv_w, out_w, fc1_w, fc2_w, vec_low = (
        lax.all_gather(shard_qkv, "fsdp", axis=0, tiled=True),
        lax.all_gather(shard_out, "fsdp", axis=0, tiled=True),
        lax.all_gather(shard_fc1, "fsdp", axis=0, tiled=True),
        lax.all_gather(shard_fc2, "fsdp", axis=0, tiled=True),
        lax.all_gather(shard_vec, "fsdp", axis=1, tiled=True),
    )
    vector_rows = vec_low.astype(jnp.float32)
    is_image = lax.broadcasted_iota(jnp.int32, (length, 1), 0) >= TEXT
    stream_zero = tokens.astype(jnp.float32) + jnp.where(is_image, vector_rows[1], vector_rows[0])
    stream_zero = stream_zero.reshape(token_rows, model_width)
    normed_one, scale_one = normalize(stream_zero)
    input_one = (normed_one * vector_rows[2] + vector_rows[3]).astype(jnp.bfloat16)
    qkv_bias = jnp.concatenate(
        [vector_rows[4], jnp.zeros((model_width,), jnp.float32), vector_rows[5]]
    )
    qkv_all = (jnp.dot(input_one, qkv_w, preferred_element_type=jnp.float32) + qkv_bias).astype(
        jnp.bfloat16
    )
    head_view = qkv_all.reshape(pair_count, length, 3, HEADS, HDIM)
    queries = head_view[:, :, 0]
    keys_all = head_view[:, :, 1]
    values_all = head_view[:, :, 2]
    scores = (
        jnp.einsum("pqhe,pkhe->pqhk", queries, keys_all, preferred_element_type=jnp.float32)
        * attn_scale
    )
    row_max = jnp.max(scores, axis=-1, keepdims=True)
    log_total = row_max + jnp.log(jnp.sum(jnp.exp(scores - row_max), axis=-1, keepdims=True))
    attn_low = jnp.exp(scores - log_total).astype(jnp.bfloat16)
    mixed_heads = jnp.einsum(
        "pqhk,pkhe->pqhe", attn_low, values_all, preferred_element_type=jnp.float32
    )
    mixed_heads = mixed_heads.astype(jnp.bfloat16).reshape(token_rows, model_width)
    stream_one = (
        stream_zero
        + jnp.dot(mixed_heads, out_w, preferred_element_type=jnp.float32)
        + vector_rows[6]
    )
    normed_two, scale_two = normalize(stream_one)
    input_two = (normed_two * vector_rows[7] + vector_rows[8]).astype(jnp.bfloat16)
    preact = jnp.dot(input_two, fc1_w, preferred_element_type=jnp.float32) + vector_rows[
        9 : 9 + fc1_parts
    ].reshape(FF)
    activated = jax.nn.gelu(preact, approximate=False).astype(jnp.bfloat16)
    result = (
        stream_one
        + jnp.dot(activated, fc2_w, preferred_element_type=jnp.float32)
        + vector_rows[9 + fc1_parts]
    )
    layer_out = result.astype(jnp.bfloat16).reshape(pair_count, length, model_width)
    qkv_w, out_w, fc1_w, fc2_w, vec_low = (
        lax.all_gather(shard_qkv, "fsdp", axis=0, tiled=True),
        lax.all_gather(shard_out, "fsdp", axis=0, tiled=True),
        lax.all_gather(shard_fc1, "fsdp", axis=0, tiled=True),
        lax.all_gather(shard_fc2, "fsdp", axis=0, tiled=True),
        lax.all_gather(shard_vec, "fsdp", axis=1, tiled=True),
    )
    vector_rows = vec_low.astype(jnp.float32)
    slot_index = lax.broadcasted_iota(jnp.int32, (pair_count, MAXM), 1)
    slot_live = slot_index < mask_count[:, None]
    positions = lax.broadcasted_iota(jnp.int32, (pair_count, MAXM, length), 2)
    keep_rows = jnp.any((mask_pos[:, :, None] == positions) & slot_live[:, :, None], axis=1)
    chosen = keep_rows.shape[1]
    picked = pair_count * chosen

    def select(values):
        shaped = values.reshape((pair_count, length) + values.shape[1:])
        return shaped.reshape((picked,) + values.shape[1:])

    def spread_back(values):
        shaped = values.reshape((pair_count, chosen) + values.shape[1:])
        return shaped.reshape((token_rows,) + values.shape[1:])

    grad_out = select(
        cotangent.reshape(token_rows, model_width).astype(jnp.float32)
    ) * keep_rows.reshape(picked, 1).astype(jnp.float32)
    grad_low = grad_out.astype(jnp.bfloat16)
    grad_fc2 = dot_first(select(activated), grad_low)
    bias_fc2 = jnp.sum(grad_out, axis=0)
    grad_act = dot_last(grad_low, fc2_w)
    preact_sel = select(preact)
    gelu_slope = (
        0.5 * (1.0 + lax.erf(preact_sel * INV_ROOT_TWO))
        + preact_sel * jnp.exp(-0.5 * preact_sel * preact_sel) * INV_ROOT_TWOPI
    )
    grad_pre = grad_act * gelu_slope
    bias_fc1 = jnp.sum(grad_pre, axis=0)
    pre_low = grad_pre.astype(jnp.bfloat16)
    grad_fc1 = dot_first(select(input_two), pre_low)
    grad_norm_two = dot_last(pre_low, fc1_w)
    normed_two_sel = select(normed_two)
    gain_two = jnp.sum(grad_norm_two * normed_two_sel, axis=0)
    shift_two = jnp.sum(grad_norm_two, axis=0)
    grad_stream = grad_out + norm_back(
        grad_norm_two, normed_two_sel, select(scale_two), vector_rows[7]
    )
    bias_out = jnp.sum(grad_stream, axis=0)
    stream_low = grad_stream.astype(jnp.bfloat16)
    grad_outw = dot_first(select(mixed_heads), stream_low)
    grad_mixed = (
        dot_last(stream_low, out_w).astype(jnp.bfloat16).reshape(pair_count, chosen, HEADS, HDIM)
    )
    queries_sel = select(queries.reshape(token_rows, HEADS, HDIM)).reshape(
        pair_count, chosen, HEADS, HDIM
    )
    total_sel = select(log_total.reshape(token_rows, HEADS, 1)).reshape(
        pair_count, chosen, HEADS, 1
    )
    scores_again = (
        jnp.einsum("pqhe,pkhe->pqhk", queries_sel, keys_all, preferred_element_type=jnp.float32)
        * attn_scale
    )
    attn_again = jnp.exp(scores_again - total_sel)
    grad_values = jnp.einsum(
        "pqhk,pqhe->pkhe",
        attn_again.astype(jnp.bfloat16),
        grad_mixed,
        preferred_element_type=jnp.float32,
    )
    grad_attn = jnp.einsum(
        "pqhe,pkhe->pqhk", grad_mixed, values_all, preferred_element_type=jnp.float32
    )
    grad_scores = attn_again * (grad_attn - jnp.sum(attn_again * grad_attn, axis=-1, keepdims=True))
    grad_scores = grad_scores.astype(jnp.bfloat16)
    grad_queries = (
        jnp.einsum("pqhk,pkhe->pqhe", grad_scores, keys_all, preferred_element_type=jnp.float32)
        * attn_scale
    )
    grad_keys = (
        jnp.einsum("pqhk,pqhe->pkhe", grad_scores, queries_sel, preferred_element_type=jnp.float32)
        * attn_scale
    )
    grad_queries = spread_back(grad_queries.reshape(picked, model_width))
    grad_values = grad_values.reshape(token_rows, model_width)
    grad_qkv = jnp.concatenate(
        [grad_queries, grad_keys.reshape(token_rows, model_width), grad_values], axis=1
    )
    bias_query = jnp.sum(grad_queries, axis=0)
    bias_value = jnp.sum(grad_values, axis=0)
    qkv_low = grad_qkv.astype(jnp.bfloat16)
    grad_qkvw = dot_first(input_one, qkv_low)
    grad_norm_one = dot_last(qkv_low, qkv_w)
    gain_one = jnp.sum(grad_norm_one * normed_one, axis=0)
    shift_one = jnp.sum(grad_norm_one, axis=0)
    grad_input = spread_back(grad_stream) + norm_back(
        grad_norm_one, normed_one, scale_one, vector_rows[2]
    )
    grad_shaped = grad_input.reshape(pair_count, length, model_width)
    type_text = jnp.sum(jnp.where(is_image, 0.0, grad_shaped), axis=(0, 1))
    type_image = jnp.sum(jnp.where(is_image, grad_shaped, 0.0), axis=(0, 1))
    grad_vec = jnp.concatenate(
        [
            jnp.stack(
                [
                    type_text,
                    type_image,
                    gain_one,
                    shift_one,
                    bias_query,
                    bias_value,
                    bias_out,
                    gain_two,
                    shift_two,
                ]
            ),
            bias_fc1.reshape(fc1_parts, model_width),
            bias_fc2[None, :],
        ],
        axis=0,
    )
    halfway = (
        lax.psum_scatter(
            grad_qkvw.astype(jnp.bfloat16), "fsdp", scatter_dimension=0, tiled=True
        ).astype(jnp.float32),
        lax.psum_scatter(
            grad_outw.astype(jnp.bfloat16), "fsdp", scatter_dimension=0, tiled=True
        ).astype(jnp.float32),
        lax.psum_scatter(
            grad_fc1.astype(jnp.bfloat16), "fsdp", scatter_dimension=0, tiled=True
        ).astype(jnp.float32),
        lax.psum_scatter(
            grad_fc2.astype(jnp.bfloat16), "fsdp", scatter_dimension=0, tiled=True
        ).astype(jnp.float32),
        lax.psum_scatter(
            grad_vec.astype(jnp.bfloat16), "fsdp", scatter_dimension=1, tiled=True
        ).astype(jnp.float32),
    )
    owned = (
        lax.psum_scatter(halfway[0], "batch", scatter_dimension=0, tiled=True),
        lax.psum_scatter(halfway[1], "batch", scatter_dimension=0, tiled=True),
        lax.psum_scatter(halfway[2], "batch", scatter_dimension=0, tiled=True),
        lax.psum_scatter(halfway[3], "batch", scatter_dimension=0, tiled=True),
        lax.psum_scatter(halfway[4], "batch", scatter_dimension=1, tiled=True),
    )
    batch_index = lax.axis_index("batch")
    masters = (w_qkv, w_out, w_fc1, w_fc2, vectors)
    firsts = (m_qkv, m_out, m_fc1, m_fc2, m_vec)
    seconds = (v_qkv, v_out, v_fc1, v_fc2, v_vec)
    alongs = (0, 0, 0, 0, 1)
    updated = []
    for master, gradient, moment_one, moment_two, along, step_rate, decay_rate in zip(
        masters, owned, firsts, seconds, alongs, STEP_RATES, DECAY_RATES
    ):
        slice_rows = gradient.shape[along]
        own_slice = lax.dynamic_slice_in_dim(master, batch_index * slice_rows, slice_rows, along)
        updated.append(adamw(own_slice, gradient, moment_one, moment_two, step_rate, decay_rate))
    new_masters = (
        lax.all_gather(updated[0][0].astype(jnp.bfloat16), "batch", axis=0, tiled=True).astype(
            jnp.float32
        ),
        lax.all_gather(updated[1][0].astype(jnp.bfloat16), "batch", axis=0, tiled=True).astype(
            jnp.float32
        ),
        lax.all_gather(updated[2][0].astype(jnp.bfloat16), "batch", axis=0, tiled=True).astype(
            jnp.float32
        ),
        lax.all_gather(updated[3][0].astype(jnp.bfloat16), "batch", axis=0, tiled=True).astype(
            jnp.float32
        ),
        lax.all_gather(updated[4][0].astype(jnp.bfloat16), "batch", axis=1, tiled=True).astype(
            jnp.float32
        ),
    )
    return (
        layer_out,
        grad_shaped,
        new_masters[0],
        updated[0][1],
        updated[0][2],
        new_masters[1],
        updated[1][1],
        updated[1][2],
        new_masters[2],
        updated[2][1],
        updated[2][2],
        new_masters[3],
        updated[3][1],
        updated[3][2],
        new_masters[4],
        updated[4][1],
        updated[4][2],
    )


def solution(mesh):
    placed = (
        P(("batch", "fsdp"), None, None),
        P(("batch", "fsdp"), None, None),
        P(("batch", "fsdp"), None),
        P(("batch", "fsdp")),
        P("fsdp", None),
        P(("fsdp", "batch"), None),
        P(("fsdp", "batch"), None),
        P("fsdp", None),
        P(("fsdp", "batch"), None),
        P(("fsdp", "batch"), None),
        P("fsdp", None),
        P(("fsdp", "batch"), None),
        P(("fsdp", "batch"), None),
        P("fsdp", None),
        P(("fsdp", "batch"), None),
        P(("fsdp", "batch"), None),
        P(None, "fsdp"),
        P(None, ("fsdp", "batch")),
        P(None, ("fsdp", "batch")),
    )
    return jax.shard_map(
        shards,
        mesh=mesh,
        in_specs=placed,
        out_specs=(
            P(("batch", "fsdp"), None, None),
            P(("batch", "fsdp"), None, None),
            P("fsdp", None),
            P(("fsdp", "batch"), None),
            P(("fsdp", "batch"), None),
            P("fsdp", None),
            P(("fsdp", "batch"), None),
            P(("fsdp", "batch"), None),
            P("fsdp", None),
            P(("fsdp", "batch"), None),
            P(("fsdp", "batch"), None),
            P("fsdp", None),
            P(("fsdp", "batch"), None),
            P(("fsdp", "batch"), None),
            P(None, "fsdp"),
            P(None, ("fsdp", "batch")),
            P(None, ("fsdp", "batch")),
        ),
        check_vma=False,
    )
```

profile of v0, /device:TPU:0, one launch (start us, length us, event | category | flops | bytes accessed | tf_op | source)
XLA Modules:
  0.0 737.7 jit_solution(3257606192598027593)
XLA Ops:
  29.4 14.3 %all-gather.9.cloned.1.call-done = bf16[768,2304]{1,0:T(8,128)(2,1)} async-done(((bf16[192,2304]{1,0:T(8,128)(2,1)}), bf16[768,2304]{1,0:T(8,128)(2,1)}) %all-gather.9.cloned.1.call-update) | async-done | bytes 3538960 | tf_op jit(solution)/shard_map/all_gather | solution.py:94
  58.9 8.9 %reshape.233 = bf16[4,256,3,12,64]{1,0,4,3,2:T(4,128)(2,1)} reshape(bf16[1024,2304]{0,1:T(8,128)(2,1)} %copy.97) | data formatting | bytes 9437184 | tf_op jit(solution)/shard_map/reshape | solution.py:112
  88.6 14.3 %all-gather.13.cloned.1.call-done = bf16[768,3072]{1,0:T(8,128)(2,1)} async-done(((bf16[192,3072]{1,0:T(8,128)(2,1)}), bf16[768,3072]{1,0:T(8,128)(2,1)}) %all-gather.13.cloned.1.call-update) | async-done | bytes 4718608 | tf_op jit(solution)/shard_map/all_gather | solution.py:96
  102.9 37.7 %fusion.2 = (bf16[1024,3072]{1,0:T(8,128)(2,1)}, f32[1024,3072]{1,0:T(8,128)}) fusion(f32[3072]{0:T(1024)S(1)} %add.230, bf16[768,3072]{1,0:T(8,128)(2,1)} %all-gather.13.cloned.1.call-done, f32[1024,768]{1,0:T(8,128)} %copy-done.12, f32[768]{0:T(1024)S(1)} %get-tuple-element.28, f32[768]{0:T(1024)S(1)} %get-tuple-element.29, f32[1024]{0:T(1024)S(1)} %add_rsqrt_fusion, ...), kind=kOutput, calls=%fused_computation.4 | convolution fusion | flops 5043388416 | bytes 26765312 | tf_op jit(solution)/shard_map/dot_general | solution.py:134
  141.7 11.9 %fusion.62 = (bf16[3072]{0:T(1024)(128)(2,1)S(1)}, bf16[1024,3072]{1,0:T(8,128)(2,1)S(1)}) fusion(f32[1024,3072]{1,0:T(8,128)} %get-tuple-element.69, f32[3072]{0:T(1024)S(1)} %add.230, bf16[1024,768]{1,0:T(8,128)(2,1)S(1)} %copy-done.23, bf16[3072,768]{1,0:T(8,128)(2,1)} %all-gather.15.cloned.1.call-done), kind=kOutput, calls=%fused_computation.151 | convolution fusion | flops 4869583872 | bytes 25184256 | tf_op jit(solution)/shard_map/dot_general | solution.py:30
  164.2 9.7 %convolution_convert_fusion = bf16[3072,768]{1,0:T(8,128)(2,1)} fusion(bf16[1024,3072]{1,0:T(8,128)(2,1)} %get-tuple-element.68, bf16[1024,768]{1,0:T(8,128)(2,1)S(1)} %copy-done.23), kind=kOutput, calls=%fused_computation.38 | convolution fusion | flops 4834197504 | bytes 12582912 | tf_op jit(solution)/shard_map/dot_general | solution.py:24
  174.0 10.4 %multiply_reduce_fusion.1 = (bf16[768]{0:T(1024)(128)(2,1)S(1)}, f32[1024]{0:T(1024)S(1)}, f32[1024]{0:T(1024)S(1)}, bf16[768]{0:T(1024)(128)(2,1)S(1)}, f32[1024,768]{1,0:T(8,128)S(1)}) fusion(f32[1024,768]{1,0:T(8,128)} %copy-done.12, f32[1024]{0:T(1024)S(1)} %add_rsqrt_fusion, f32[1024]{0:T(1024)S(1)} %broadcast_multiply_fusion.4, ...), kind=kOutput, calls=%fused_computation.51 | convolution fusion | flops 4838912000 | bytes 17324032 | tf_op jit(solution)/shard_map/dot_general | solution.py:30
  191.0 8.7 %bitcast_convert_fusion = (bf16[4,256,12,64]{1,3,2,0:T(8,128)(2,1)S(1)}, f32[4,12,64,256]{3,2,1,0:T(8,128)}) fusion(f32[4,12,256,256]{3,2,1,0:T(8,128)} %copy-done, f32[4,256,12]{1,2,0:T(8,128)S(1)} %log_add_fusion, bf16[4,256,12,64]{1,0,3,2:T(4,128)(2,1)S(1)} %reshape.236), kind=kOutput, calls=%fused_computation.42 | convolution fusion | flops 412876800 | bytes 18923520 | tf_op jit(solution)/shard_map/pqhk,pqhe->pkhe/dot_general | solution.py:207
  204.9 9.0 %fusion.8 = (f32[4,256,12]{1,2,0:T(8,128)S(1)}, f32[4,12,256,256]{3,2,1,0:T(8,128)}) fusion(f32[4,12,256,256]{3,2,1,0:T(8,128)} %copy-done, f32[4,256,12]{1,2,0:T(8,128)S(1)} %log_add_fusion, bf16[4,256,12,64]{1,0,3,2:T(4,128)(2,1)S(1)} %reshape.236, bf16[4,256,1,12,64]{1,0,4,3,2:T(4,128)(2,1)S(1)} %copy-done.4), kind=kOutput, calls=%fused_computation.12 | convolution fusion | flops 415223808 | bytes 28409856 | tf_op jit(solution)/shard_map/pqhe,pkhe->pqhk/dot_general | solution.py:213
  214.0 11.4 %fusion.10 = bf16[4,256,12,256]{1,3,2,0:T(8,128)(2,1)S(1)} fusion(f32[4,12,256,256]{3,2,1,0:T(8,128)} %get-tuple-element.72, f32[4,12,256,256]{3,2,1,0:T(8,128)} %copy-done, f32[4,256,12]{1,2,0:T(8,128)S(1)} %get-tuple-element.71, f32[4,256,12]{1,2,0:T(8,128)S(1)} %log_add_fusion), kind=kLoop, calls=%fused_computation.14 | loop fusion | flops 15728640 | bytes 31555584 | tf_op jit(solution)/shard_map/convert_element_type | solution.py:217
  245.9 16.8 %reduce-scatter.25.cloned.1.call-done = bf16[768,768]{1,0:T(8,128)(2,1)} async-done(((bf16[3072,768]{1,0:T(8,128)(2,1)}), bf16[768,768]{1,0:T(8,128)(2,1)}) %reduce-scatter.25.cloned.1.call-update) | async-done | bytes 1179664 | tf_op jit(solution)/shard_map/reduce_scatter | solution.py:274
  270.8 8.8 %multiply_reduce_fusion.2 = (bf16[768]{0:T(1024)(128)(2,1)S(1)}, f32[1024]{0:T(1024)S(1)}, f32[1024]{0:T(1024)S(1)}, bf16[768]{0:T(1024)(128)(2,1)S(1)}, f32[1024,768]{1,0:T(8,128)S(1)}) fusion(f32[4,256,768]{2,1,0:T(8,128)S(1)} %copy-done.2, f32[1024]{0:T(1024)S(1)} %bitcast.176, f32[1024]{0:T(1024)S(1)} %bitcast.173, f32[768]{0:T(1024)S(1)} %copy-done.32, ...), kind=kOutput, calls=%fused_computation.52 | convolution fusion | flops 3630952960 | bytes 14571520 | tf_op jit(solution)/shard_map/dot_general | solution.py:30
  293.3 41.0 %reduce-scatter.13.cloned.1.call-done = bf16[192,2304]{1,0:T(8,128)(2,1)} async-done(((bf16[768,2304]{1,0:T(8,128)(2,1)}), bf16[192,2304]{1,0:T(8,128)(2,1)}) %reduce-scatter.13.cloned.1.call-update) | async-done | bytes 884752 | tf_op jit(solution)/shard_map/reduce_scatter | solution.py:265
  337.0 71.3 %reduce-scatter.23.cloned.1.call-done = f32[24,3072]{1,0:T(8,128)} async-done(((f32[192,3072]{1,0:T(8,128)}), f32[24,3072]{1,0:T(8,128)}) %reduce-scatter.23.cloned.1.call-update) | async-done | bytes 294928 | tf_op jit(solution)/shard_map/reduce_scatter | solution.py:284
  411.7 69.4 %reduce-scatter.27.cloned.1.call-done = f32[96,768]{1,0:T(8,128)} async-done(((f32[768,768]{1,0:T(8,128)}), f32[96,768]{1,0:T(8,128)}) %reduce-scatter.27.cloned.1.call-update) | async-done | bytes 294928 | tf_op jit(solution)/shard_map/reduce_scatter | solution.py:285
  483.5 9.5 %add_convert_fusion.1 = bf16[1024,768]{1,0:T(8,128)(2,1)} fusion(f32[1024,768]{1,0:T(8,128)S(1)} %copy-done.15, bf16[1024,3072]{1,0:T(8,128)(2,1)} %get-tuple-element.68, bf16[3072,768]{1,0:T(8,128)(2,1)} %all-gather.15.cloned.1.call-done, f32[768]{0:T(1024)S(1)} %copy-done.44), kind=kOutput, calls=%fused_computation.63 | convolution fusion | flops 4834197504 | bytes 15731712 | tf_op jit(solution)/shard_map/dot_general | solution.py:140
  492.9 10.2 %reduce-scatter.29.cloned.1.call-done = bf16[192,14]{1,0:T(8,128)(2,1)} async-done(((bf16[768,14]{1,0:T(8,128)(2,1)}), bf16[192,14]{1,0:T(8,128)(2,1)}) %reduce-scatter.29.cloned.1.call-update) | async-done | bytes 5392
  504.0 37.2 %all-reduce = f32[14,192]{1,0:T(8,128)S(1)} all-reduce(bf16[14,192]{1,0:T(8,128)(2,1)S(1)} %copy.118), channel_id=11, replica_groups=mesh['batch'=8,'fsdp'=4] {'batch'}, use_global_device_ids=true, to_apply=%region_32.33.clone | all-reduce | flops 2688 | bytes 16128
  541.9 30.7 %all-gather.1 = bf16[8,24,14]{1,2,0:T(8,128)(2,1)S(1)} all-gather(bf16[1,24,14]{1,2,0:T(8,128)(2,1)S(1)} %get-tuple-element.37), channel_id=1, replica_groups=mesh['batch'=8,'fsdp'=4] {'batch'}, dimensions={0}, use_global_device_ids=true | all-gather | bytes 6048 | tf_op jit(solution)/shard_map/all_gather | solution.py:313
  574.9 31.4 %all_gather.41 = bf16[192,768]{1,0:T(8,128)(2,1)S(1)} all-gather(bf16[24,768]{1,0:T(8,128)(2,1)S(1)} %get-tuple-element.49), channel_id=1, replica_groups=mesh['batch'=8,'fsdp'=4] {'batch'}, dimensions={0}, use_global_device_ids=true | all-gather | bytes 331776 | tf_op jit(solution)/shard_map/all_gather | solution.py:304
  607.2 32.5 %reduce-scatter.15.cloned.1.call-done = f32[24,2304]{1,0:T(8,128)} async-done(((f32[192,2304]{1,0:T(8,128)}), f32[24,2304]{1,0:T(8,128)}) %reduce-scatter.15.cloned.1.call-update) | async-done | bytes 221200 | tf_op jit(solution)/shard_map/reduce_scatter | solution.py:282
  641.7 33.8 %all_gather.40 = bf16[192,2304]{1,0:T(8,128)(2,1)S(1)} all-gather(bf16[24,2304]{1,0:T(8,128)(2,1)S(1)} %get-tuple-element.52), channel_id=1, replica_groups=mesh['batch'=8,'fsdp'=4] {'batch'}, dimensions={0}, use_global_device_ids=true | all-gather | bytes 995328 | tf_op jit(solution)/shard_map/all_gather | solution.py:301
  676.8 8.8 %all-gather.17.cloned.1.call-done = bf16[192,3072]{1,0:T(8,128)(2,1)} async-done(((bf16[24,3072]{1,0:T(8,128)(2,1)}), bf16[192,3072]{1,0:T(8,128)(2,1)}) %all-gather.17.cloned.1.call-update) | async-done | bytes 1179664 | tf_op jit(solution)/shard_map/all_gather | solution.py:307
  688.6 39.3 %all-gather.19.cloned.1.call-done = bf16[768,768]{1,0:T(8,128)(2,1)} async-done(((bf16[96,768]{1,0:T(8,128)(2,1)}), bf16[768,768]{1,0:T(8,128)(2,1)}) %all-gather.19.cloned.1.call-update) | async-done | bytes 1179664 | tf_op jit(solution)/shard_map/all_gather | solution.py:310
  (236 shorter events, 144.8 us)
Async XLA Ops:
  7.2 36.4 %all-gather.9.cloned.1.call-start = ((), (), s32[]{:S(2)}) async-start(), calls=%async_computation.9 | async-start | bytes 4423680 | tf_op jit(solution)/shard_map/all_gather | solution.py:94
  9.9 73.0 %all-gather.11.cloned.1.call-start = ((), (), s32[]{:S(2)}) async-start(), calls=%async_computation.10 | async-start | bytes 1474560 | tf_op jit(solution)/shard_map/all_gather | solution.py:95
  10.7 92.1 %all-gather.13.cloned.1.call-start = ((), (), s32[]{:S(2)}) async-start(), calls=%async_computation.11 | async-start | bytes 5898240 | tf_op jit(solution)/shard_map/all_gather | solution.py:96
  12.0 129.7 %all-gather.15.cloned.1.call-start = ((), (), s32[]{:S(2)}) async-start(), calls=%async_computation.12 | async-start | bytes 5898240 | tf_op jit(solution)/shard_map/all_gather | solution.py:97
  15.0 227.8 %reduce-scatter.21.cloned.1.call-start = ((), (), s32[]{:S(2)}) async-start(), calls=%async_computation.17 | async-start | bytes 5898240 | tf_op jit(solution)/shard_map/reduce_scatter | solution.py:271
  164.1 98.5 %reduce-scatter.25.cloned.1.call-start = ((), (), s32[]{:S(2)}) async-start(), calls=%async_computation.20 | async-start | bytes 5898240 | tf_op jit(solution)/shard_map/reduce_scatter | solution.py:274
  174.0 117.5 %reduce-scatter.17.cloned.1.call-start = ((), (), s32[]{:S(2)}) async-start(), calls=%async_computation.15 | async-start | bytes 1474560 | tf_op jit(solution)/shard_map/reduce_scatter | solution.py:268
  213.9 120.5 %reduce-scatter.13.cloned.1.call-start = ((), (), s32[]{:S(2)}) async-start(), calls=%async_computation.13 | async-start | bytes 4423680 | tf_op jit(solution)/shard_map/reduce_scatter | solution.py:265
  242.7 165.5 %reduce-scatter.23.cloned.1.call-start = ((), (), s32[]{:S(2)}) async-start(), calls=%async_computation.18 | async-start | bytes 2654208 | tf_op jit(solution)/shard_map/reduce_scatter | solution.py:284
  245.8 235.3 %reduce-scatter.27.cloned.1.call-start = ((), (), s32[]{:S(2)}) async-start(), calls=%async_computation.21 | async-start | bytes 2654208 | tf_op jit(solution)/shard_map/reduce_scatter | solution.py:285
  265.5 237.6 %reduce-scatter.29.cloned.1.call-start = ((), (), s32[]{:S(2)}) async-start(), calls=%async_computation.23 | async-start | bytes 245760
  282.8 125.5 %copy-start.27 = (f32[24,3072]{1,0:T(8,128)S(1)}, f32[24,3072]{1,0:T(8,128)}, u32[]{:S(2)}) copy-start(f32[24,3072]{1,0:T(8,128)} %param.30) | copy-start | bytes 884740
  283.7 289.6 %reduce-scatter.19.cloned.1.call-start = ((), (), s32[]{:S(2)}) async-start(), calls=%async_computation.16 | async-start | bytes 663552 | tf_op jit(solution)/shard_map/reduce_scatter | solution.py:283
  293.3 117.2 %copy-start.50 = (u32[32]{0:T(128)S(1)}, u32[32]{0:T(128)}, u32[]{:S(2)}) copy-start(u32[32]{0:T(128)} %constant.159) | copy-start | bytes 388
  293.3 346.4 %reduce-scatter.15.cloned.1.call-start = ((), (), s32[]{:S(2)}) async-start(), calls=%async_computation.14 | async-start | bytes 1990656 | tf_op jit(solution)/shard_map/reduce_scatter | solution.py:282
  336.9 146.5 %copy-start.15 = (f32[1024,768]{1,0:T(8,128)S(1)}, f32[1024,768]{1,0:T(8,128)}, u32[]{:S(2)}) copy-start(f32[1024,768]{1,0:T(8,128)} %copy-done.12) | copy-start | bytes 9437188
  336.9 146.5 %copy-start.44 = (f32[768]{0:T(1024)S(1)}, f32[768]{0:T(1024)}, u32[]{:S(2)}) copy-start(f32[768]{0:T(1024)} %get-tuple-element.27) | copy-start | bytes 9220
  336.9 348.7 %all-gather.17.cloned.1.call-start = ((), (), s32[]{:S(2)}) async-start(), calls=%async_computation.19 | async-start | bytes 1327104 | tf_op jit(solution)/shard_map/all_gather | solution.py:307
  410.4 317.4 %all-gather.19.cloned.1.call-start = ((), (), s32[]{:S(2)}) async-start(), calls=%async_computation.22 | async-start | bytes 1327104 | tf_op jit(solution)/shard_map/all_gather | solution.py:310
  483.4 57.8 %copy-start.40 = (f32[14,192]{1,0:T(8,128)S(1)}, f32[14,192]{1,0:T(8,128)}, u32[]{:S(2)}) copy-start(f32[14,192]{1,0:T(8,128)} %param.35) | copy-start | bytes 32260
  483.4 57.8 %copy-start.42 = (f32[14,24]{1,0:T(8,128)S(1)}, f32[14,24]{1,0:T(8,128)}, u32[]{:S(2)}) copy-start(f32[14,24]{1,0:T(8,128)} %param.36) | copy-start | bytes 4036
  483.4 89.9 %copy-start.29 = (f32[24,768]{1,0:T(8,128)S(1)}, f32[24,768]{1,0:T(8,128)}, u32[]{:S(2)}) copy-start(f32[24,768]{1,0:T(8,128)} %param.27) | copy-start | bytes 221188
  483.4 89.9 %copy-start.30 = (f32[24,768]{1,0:T(8,128)S(1)}, f32[24,768]{1,0:T(8,128)}, u32[]{:S(2)}) copy-start(f32[24,768]{1,0:T(8,128)} %param.28) | copy-start | bytes 221188
  483.5 156.2 %copy-start.28 = (f32[24,2304]{1,0:T(8,128)S(1)}, f32[24,2304]{1,0:T(8,128)}, u32[]{:S(2)}) copy-start(f32[24,2304]{1,0:T(8,128)} %param.24) | copy-start | bytes 663556
  (43 other events, 403.0 us)
Sparse Core Ops, SparseCore 0:
  10.2 33.4 all-gather.8
  45.8 17.4 all-gather.10
  65.4 37.4 all-gather.12
  104.3 37.4 all-gather.14
  164.2 47.9 reduce-scatter.20
  214.6 47.9 reduce-scatter.24
  265.8 25.6 reduce-scatter.16
  294.0 40.3 reduce-scatter.12
  338.5 69.7 reduce-scatter.22
  412.2 68.8 reduce-scatter.26
  484.2 18.9 reduce-scatter.28
  506.9 62.8 reduce-scatter.18
  573.8 65.7 reduce-scatter.14
  642.3 43.3 all-gather.16
  687.7 40.1 all-gather.18
where the time goes:
time: 744 us; the launch traced here: 738 us
  waiting for transfers between devices  327 us (44%)
  matrix products  144 us (19%)
  blocking collectives  139 us (19%)
  other arithmetic  65.4 us (9%)
  local copies, waits for them, and re-layouts  45.8 us (6%)
  between operations  16 us (2%)
    reduce_scatter x1, waiting for transfers between devices, shards(): lax.psum_scatter(halfway[2], 'batch', scatter_dimension=0, tiled=True)  71.3 us
    reduce_scatter x1, waiting for transfers between devices, shards(): lax.psum_scatter(halfway[3], 'batch', scatter_dimension=0, tiled=True)  69.4 us
    reduce_scatter x1, waiting for transfers between devices, shards(): lax.psum_scatter(grad_qkvw.astype(jnp.bfloat16), 'fsdp', scatter_dimensio...  41 us
    all_gather x1, waiting for transfers between devices, shards(): lax.all_gather(updated[3][0].astype(jnp.bfloat16), 'batch', axis=0, tiled...  39.3 us
    dot_general x1, matrix products, shards(): jnp.dot(input_two, fc1_w, preferred_element_type=jnp.float32)  37.7 us
    unnamed x1, blocking collectives  37.2 us
    all_gather x1, blocking collectives, shards(): lax.all_gather(updated[0][0].astype(jnp.bfloat16), 'batch', axis=0, tiled...  33.8 us
    reduce_scatter x1, waiting for transfers between devices, shards(): lax.psum_scatter(halfway[0], 'batch', scatter_dimension=0, tiled=True)  32.5 us
  transfers between devices with their start and end apart: 15, of which 12 were waited for; matrix products, arithmetic and copies ran while one was open for 30% of the time, Pallas kernels for 0%

commit v1 on v0

--- a/solution.py
+++ b/solution.py
@@ -18,6 +18,28 @@
 DECAY_RATES = (0.01, 0.01, 0.01, 0.01, 0.0)
 INV_ROOT_TWO = 1.0 / math.sqrt(2.0)
 INV_ROOT_TWOPI = 1.0 / math.sqrt(2.0 * math.pi)
+
+
+def joined_along(parts, dim):
+    lengths = list(parts.shape[1:])
+    lengths[dim] *= parts.shape[0]
+    return jnp.moveaxis(parts, 0, dim).reshape(lengths)
+
+
+def grow_blocks(x, axis):
+    count = lax.axis_size(axis)
+    parts = x[None]
+    for level in range(count.bit_length() - 1):
+        bit = 1 << level
+        theirs = lax.ppermute(parts, axis, [(i, i ^ bit) for i in range(count)])
+        both = jnp.stack([parts, theirs])
+        upper = lax.axis_index(axis) >> level & 1
+        parts = jnp.where(upper == 0, both, both[::-1]).reshape(-1, *x.shape)
+    return parts
+
+
+def doubled_up(shard, axis, dim):
+    return joined_along(grow_blocks(shard, axis), dim)
 
 
 def dot_first(left_mat, right_mat):
@@ -307,9 +329,7 @@
         lax.all_gather(updated[2][0].astype(jnp.bfloat16), "batch", axis=0, tiled=True).astype(
             jnp.float32
         ),
-        lax.all_gather(updated[3][0].astype(jnp.bfloat16), "batch", axis=0, tiled=True).astype(
-            jnp.float32
-        ),
+        doubled_up(updated[3][0].astype(jnp.bfloat16), "batch", 0).astype(jnp.float32),
         lax.all_gather(updated[4][0].astype(jnp.bfloat16), "batch", axis=1, tiled=True).astype(
             jnp.float32
         ),

time: 744 us -> 696 us (0.935)
  waiting for transfers between devices: 327 us -> 275 us
    reduce_scatter x1, waiting for transfers between devices: 69.4 us -> 3.43 us  [shards(): lax.psum_scatter(halfway[3], 'batch', scatter_dimension=0, tiled=True)]
    reduce_scatter x1, waiting for transfers between devices: 0.01 us -> 63.1 us  [shards(): lax.psum_scatter(halfway[1], 'batch', scatter_dimension=0, tiled=True)]
    reduce_scatter x1, waiting for transfers between devices: 32.5 us -> 73.6 us  [shards(): lax.psum_scatter(halfway[0], 'batch', scatter_dimension=0, tiled=True)]
    all_gather x1 -> x0, waiting for transfers between devices: 39.3 us -> none  [shards(): lax.all_gather(updated[3][0].astype(jnp.bfloat16), 'batch', axis=0, tiled...]
    reduce_scatter x1, waiting for transfers between devices: 71.3 us -> 40.5 us  [shards(): lax.psum_scatter(halfway[2], 'batch', scatter_dimension=0, tiled=True)]
    reduce_scatter x1, waiting for transfers between devices: 16.8 us -> 0.02 us  [shards(): lax.psum_scatter(grad_fc2.astype(jnp.bfloat16), 'fsdp', scatter_dimension...]
    reduce_scatter x1, waiting for transfers between devices: 0.02 us -> 9.7 us  [shards(): lax.psum_scatter(grad_fc1.astype(jnp.bfloat16), 'fsdp', scatter_dimension...]
    reduce_scatter x1, waiting for transfers between devices: 7.7 us -> 0.02 us  [shards(): lax.psum_scatter(grad_outw.astype(jnp.bfloat16), 'fsdp', scatter_dimensio...]
  transfers between devices with their start and end apart: 15 -> 17, of which waited for: 12 -> 10; matrix products, arithmetic and copies ran while one was open for 30% -> 35% of each run, Pallas kernels for 0% -> 0%
where the time goes in v1:
time: 696 us; the launch traced here: 690 us
  waiting for transfers between devices  275 us (40%)
  matrix products  147 us (21%)
  blocking collectives  141 us (20%)
  other arithmetic  61.2 us (9%)
  local copies, waits for them, and re-layouts  47.6 us (7%)
  between operations  16 us (2%)
    reduce_scatter x1, waiting for transfers between devices, shards(): lax.psum_scatter(halfway[0], 'batch', scatter_dimension=0, tiled=True)  73.6 us
    reduce_scatter x1, waiting for transfers between devices, shards(): lax.psum_scatter(halfway[1], 'batch', scatter_dimension=0, tiled=True)  63.1 us
    reduce_scatter x1, waiting for transfers between devices, shards(): lax.psum_scatter(halfway[2], 'batch', scatter_dimension=0, tiled=True)  40.5 us
    reduce_scatter x1, waiting for transfers between devices, shards(): lax.psum_scatter(grad_qkvw.astype(jnp.bfloat16), 'fsdp', scatter_dimensio...  38.4 us
    unnamed x1, blocking collectives  37.7 us
    dot_general x1, matrix products, shards(): jnp.dot(input_two, fc1_w, preferred_element_type=jnp.float32)  36.9 us
    dot_general x4, matrix products, dot_last(): lax.dot_general(left_mat, right_mat, (((1,), (1,)), ((), ())), preferred_...  34.7 us
    all_gather x1, blocking collectives, shards(): lax.all_gather(updated[0][0].astype(jnp.bfloat16), 'batch', axis=0, tiled...  34.1 us
  transfers between devices with their start and end apart: 17, of which 10 were waited for; matrix products, arithmetic and copies ran while one was open for 35% of the time, Pallas kernels for 0%

profile of v1, /device:TPU:0, one launch (start us, length us, event | category | flops | bytes accessed | tf_op | source)
XLA Modules:
  0.0 690.5 jit_solution(1789816122157430045)
XLA Ops:
  29.4 14.2 %all-gather.8.cloned.1.call-done = bf16[768,2304]{1,0:T(8,128)(2,1)} async-done(((bf16[192,2304]{1,0:T(8,128)(2,1)}), bf16[768,2304]{1,0:T(8,128)(2,1)}) %all-gather.8.cloned.1.call-update) | async-done | bytes 3538960 | tf_op jit(solution)/shard_map/all_gather | solution.py:116
  43.6 8.4 %add_convert_fusion = bf16[1024,2304]{1,0:T(8,128)(2,1)} fusion(bf16[1024,768]{1,0:T(8,128)(2,1)} %add_convert_fusion.3, bf16[768,2304]{1,0:T(8,128)(2,1)} %all-gather.8.cloned.1.call-done, f32[2304]{0:T(1024)S(1)} %pad_maximum_fusion.3), kind=kOutput, calls=%fused_computation.36 | convolution fusion | flops 3628597248 | bytes 9839616 | tf_op jit(solution)/shard_map/dot_general | solution.py:131
  52.1 7.2 %copy.97 = bf16[1024,2304]{0,1:T(8,128)(2,1)} copy(bf16[1024,2304]{1,0:T(8,128)(2,1)} %add_convert_fusion) | data formatting | bytes 9437184 | tf_op jit(solution)/shard_map/convert_element_type | solution.py:131
  59.3 8.9 %reshape.241 = bf16[4,256,3,12,64]{1,0,4,3,2:T(4,128)(2,1)} reshape(bf16[1024,2304]{0,1:T(8,128)(2,1)} %copy.97) | data formatting | bytes 9437184 | tf_op jit(solution)/shard_map/reshape | solution.py:134
  88.8 14.1 %all-gather.12.cloned.1.call-done = bf16[768,3072]{1,0:T(8,128)(2,1)} async-done(((bf16[192,3072]{1,0:T(8,128)(2,1)}), bf16[768,3072]{1,0:T(8,128)(2,1)}) %all-gather.12.cloned.1.call-update) | async-done | bytes 4718608 | tf_op jit(solution)/shard_map/all_gather | solution.py:118
  102.9 36.9 %fusion.2 = (bf16[1024,3072]{1,0:T(8,128)(2,1)S(1)}, f32[1024,3072]{1,0:T(8,128)}) fusion(f32[3072]{0:T(1024)S(1)} %add.230, bf16[768,3072]{1,0:T(8,128)(2,1)} %all-gather.12.cloned.1.call-done, f32[1024,768]{1,0:T(8,128)} %copy-done.11, f32[768]{0:T(1024)S(1)} %get-tuple-element.28, f32[768]{0:T(1024)S(1)} %get-tuple-element.29, ...), kind=kOutput, calls=%fused_computation.4 | convolution fusion | flops 5043388416 | bytes 26765312 | tf_op jit(solution)/shard_map/dot_general | solution.py:156
  149.4 12.3 %fusion.64 = (bf16[3072]{0:T(1024)(128)(2,1)S(1)}, bf16[1024,3072]{1,0:T(8,128)(2,1)S(1)}) fusion(f32[1024,3072]{1,0:T(8,128)} %get-tuple-element.71, f32[3072]{0:T(1024)S(1)} %add.230, bf16[1024,768]{1,0:T(8,128)(2,1)S(1)} %copy-done.18, bf16[3072,768]{1,0:T(8,128)(2,1)} %all-gather.14.cloned.1.call-done), kind=kOutput, calls=%fused_computation.160 | convolution fusion | flops 4869583872 | bytes 25184256 | tf_op jit(solution)/shard_map/dot_general | solution.py:52
  161.8 10.3 %multiply_reduce_fusion.1 = (bf16[768]{0:T(1024)(128)(2,1)S(1)}, f32[1024]{0:T(1024)S(1)}, f32[1024]{0:T(1024)S(1)}, bf16[768]{0:T(1024)(128)(2,1)S(1)}, f32[1024,768]{1,0:T(8,128)S(1)}) fusion(f32[1024,768]{1,0:T(8,128)S(1)} %copy-done.12, f32[1024]{0:T(1024)S(1)} %add_rsqrt_fusion, f32[1024]{0:T(1024)S(1)} %broadcast_multiply_fusion.4, ...), kind=kOutput, calls=%fused_computation.51 | convolution fusion | flops 4838912000 | bytes 17324032 | tf_op jit(solution)/shard_map/dot_general | solution.py:52
  177.8 10.5 %convolution_convert_fusion.1 = bf16[768,3072]{1,0:T(8,128)(2,1)} fusion(bf16[1024,3072]{1,0:T(8,128)(2,1)} %copy-done.48, f32[1024,768]{1,0:T(8,128)} %copy-done.11, f32[768]{0:T(1024)S(1)} %get-tuple-element.28, f32[768]{0:T(1024)S(1)} %get-tuple-element.29, f32[1024]{0:T(1024)S(1)} %add_rsqrt_fusion, f32[1024]{0:T(1024)S(1)} %broadcast_multiply_fusion.4), kind=kOutput, calls=%fused_computation.39 | convolution fusion | flops 4838129664 | bytes 14170112 | tf_op jit(solution)/shard_map/dot_general | solution.py:46
  197.0 8.6 %bitcast_convert_fusion = (bf16[4,256,12,64]{1,3,2,0:T(8,128)(2,1)S(1)}, f32[4,12,64,256]{3,2,1,0:T(8,128)}) fusion(f32[4,12,256,256]{3,2,1,0:T(8,128)} %copy-done, f32[4,256,12]{1,2,0:T(8,128)S(1)} %log_add_fusion, bf16[4,256,12,64]{1,0,3,2:T(4,128)(2,1)S(1)} %reshape.244), kind=kOutput, calls=%fused_computation.42 | convolution fusion | flops 412876800 | bytes 18923520 | tf_op jit(solution)/shard_map/pqhk,pqhe->pkhe/dot_general | solution.py:229
  207.2 11.5 %fusion.8 = (f32[4,256,12]{1,2,0:T(8,128)S(1)}, f32[4,12,256,256]{3,2,1,0:T(8,128)}) fusion(f32[4,12,256,256]{3,2,1,0:T(8,128)} %copy-done, f32[4,256,12]{1,2,0:T(8,128)S(1)} %log_add_fusion, bf16[4,256,12,64]{1,0,3,2:T(4,128)(2,1)S(1)} %reshape.244, bf16[4,256,1,12,64]{1,0,4,3,2:T(4,128)(2,1)S(1)} %copy-done.4), kind=kOutput, calls=%fused_computation.12 | convolution fusion | flops 415223808 | bytes 28409856 | tf_op jit(solution)/shard_map/pqhe,pkhe->pqhk/dot_general | solution.py:235
  219.1 7.4 %fusion.10 = bf16[4,256,12,256]{1,3,2,0:T(8,128)(2,1)S(1)} fusion(f32[4,12,256,256]{3,2,1,0:T(8,128)} %get-tuple-element.74, f32[4,12,256,256]{3,2,1,0:T(8,128)S(1)} %bitcast.173, f32[4,256,12]{1,2,0:T(8,128)S(1)} %get-tuple-element.73, f32[4,256,12]{1,2,0:T(8,128)S(1)} %log_add_fusion), kind=kLoop, calls=%fused_computation.14 | loop fusion | flops 15728640 | bytes 31555584 | tf_op jit(solution)/shard_map/convert_element_type | solution.py:239
  249.5 8.4 %multiply_reduce_fusion.2 = (bf16[768]{0:T(1024)(128)(2,1)S(1)}, f32[1024]{0:T(1024)S(1)}, f32[1024]{0:T(1024)S(1)}, bf16[768]{0:T(1024)(128)(2,1)S(1)}, f32[1024,768]{1,0:T(8,128)S(1)}) fusion(f32[4,256,768]{2,1,0:T(8,128)S(1)} %copy-done.2, f32[1024]{0:T(1024)S(1)} %bitcast.199, f32[1024]{0:T(1024)S(1)} %bitcast.196, f32[768]{0:T(1024)S(1)} %copy-done.30, ...), kind=kOutput, calls=%fused_computation.52 | convolution fusion | flops 3630952960 | bytes 14571520 | tf_op jit(solution)/shard_map/dot_general | solution.py:52
  267.0 9.7 %reduce-scatter.21.cloned.1.call-done = bf16[192,3072]{1,0:T(8,128)(2,1)} async-done(((bf16[768,3072]{1,0:T(8,128)(2,1)}), bf16[192,3072]{1,0:T(8,128)(2,1)}) %reduce-scatter.21.cloned.1.call-update) | async-done | bytes 1179664 | tf_op jit(solution)/shard_map/reduce_scatter | solution.py:293
  281.2 38.4 %reduce-scatter.13.cloned.1.call-done = bf16[192,2304]{1,0:T(8,128)(2,1)} async-done(((bf16[768,2304]{1,0:T(8,128)(2,1)}), bf16[192,2304]{1,0:T(8,128)(2,1)}) %reduce-scatter.13.cloned.1.call-update) | async-done | bytes 884752 | tf_op jit(solution)/shard_map/reduce_scatter | solution.py:287
  322.3 9.4 %add_convert_fusion.1 = bf16[1024,768]{1,0:T(8,128)(2,1)} fusion(f32[1024,768]{1,0:T(8,128)S(1)} %copy-done.13, bf16[1024,3072]{1,0:T(8,128)(2,1)} %copy-done.49, bf16[3072,768]{1,0:T(8,128)(2,1)} %all-gather.14.cloned.1.call-done, f32[768]{0:T(1024)S(1)} %copy-done.42), kind=kOutput, calls=%fused_computation.63 | convolution fusion | flops 4834197504 | bytes 15731712 | tf_op jit(solution)/shard_map/dot_general | solution.py:162
  331.7 10.7 %reduce-scatter.29.cloned.1.call-done = bf16[192,14]{1,0:T(8,128)(2,1)} async-done(((bf16[768,14]{1,0:T(8,128)(2,1)}), bf16[192,14]{1,0:T(8,128)(2,1)}) %reduce-scatter.29.cloned.1.call-update) | async-done | bytes 5392
  343.3 37.7 %all-reduce = f32[14,192]{1,0:T(8,128)S(1)} all-reduce(bf16[14,192]{1,0:T(8,128)(2,1)S(1)} %copy.118), channel_id=11, replica_groups=mesh['batch'=8,'fsdp'=4] {'batch'}, use_global_device_ids=true, to_apply=%region_32.33.clone | all-reduce | flops 2688 | bytes 16128
  381.7 30.8 %all-gather.1 = bf16[8,24,14]{1,2,0:T(8,128)(2,1)S(1)} all-gather(bf16[1,24,14]{1,2,0:T(8,128)(2,1)S(1)} %get-tuple-element.37), channel_id=1, replica_groups=mesh['batch'=8,'fsdp'=4] {'batch'}, dimensions={0}, use_global_device_ids=true | all-gather | bytes 6048 | tf_op jit(solution)/shard_map/all_gather | solution.py:333
  419.5 63.1 %reduce-scatter.19.cloned.1.call-done = f32[24,768]{1,0:T(8,128)} async-done(((f32[192,768]{1,0:T(8,128)}), f32[24,768]{1,0:T(8,128)}) %reduce-scatter.19.cloned.1.call-update) | async-done | bytes 73744 | tf_op jit(solution)/shard_map/reduce_scatter | solution.py:305
  484.2 31.7 %all_gather.38 = bf16[192,768]{1,0:T(8,128)(2,1)S(1)} all-gather(bf16[24,768]{1,0:T(8,128)(2,1)S(1)} %get-tuple-element.49), channel_id=1, replica_groups=mesh['batch'=8,'fsdp'=4] {'batch'}, dimensions={0}, use_global_device_ids=true | all-gather | bytes 331776 | tf_op jit(solution)/shard_map/all_gather | solution.py:326
  516.9 40.5 %reduce-scatter.23.cloned.1.call-done = f32[24,3072]{1,0:T(8,128)} async-done(((f32[192,3072]{1,0:T(8,128)}), f32[24,3072]{1,0:T(8,128)}) %reduce-scatter.23.cloned.1.call-update) | async-done | bytes 294928 | tf_op jit(solution)/shard_map/reduce_scatter | solution.py:306
  561.1 73.6 %reduce-scatter.15.cloned.1.call-done = f32[24,2304]{1,0:T(8,128)} async-done(((f32[192,2304]{1,0:T(8,128)}), f32[24,2304]{1,0:T(8,128)}) %reduce-scatter.15.cloned.1.call-update) | async-done | bytes 221200 | tf_op jit(solution)/shard_map/reduce_scatter | solution.py:304
  636.7 34.1 %all_gather.37 = bf16[192,2304]{1,0:T(8,128)(2,1)S(1)} all-gather(bf16[24,2304]{1,0:T(8,128)(2,1)S(1)} %get-tuple-element.52), channel_id=1, replica_groups=mesh['batch'=8,'fsdp'=4] {'batch'}, dimensions={0}, use_global_device_ids=true | all-gather | bytes 995328 | tf_op jit(solution)/shard_map/all_gather | solution.py:323
  (248 shorter events, 135.9 us)
Async XLA Ops:
  7.2 36.4 %all-gather.8.cloned.1.call-start = ((), (), s32[]{:S(2)}) async-start(), calls=%async_computation.9 | async-start | bytes 4423680 | tf_op jit(solution)/shard_map/all_gather | solution.py:116
  9.9 73.3 %all-gather.10.cloned.1.call-start = ((), (), s32[]{:S(2)}) async-start(), calls=%async_computation.10 | async-start | bytes 1474560 | tf_op jit(solution)/shard_map/all_gather | solution.py:117
  10.7 92.1 %all-gather.12.cloned.1.call-start = ((), (), s32[]{:S(2)}) async-start(), calls=%async_computation.11 | async-start | bytes 5898240 | tf_op jit(solution)/shard_map/all_gather | solution.py:118
  12.0 137.4 %all-gather.14.cloned.1.call-start = ((), (), s32[]{:S(2)}) async-start(), calls=%async_computation.12 | async-start | bytes 5898240 | tf_op jit(solution)/shard_map/all_gather | solution.py:119
  15.0 247.1 %reduce-scatter.25.cloned.1.call-start = ((), (), s32[]{:S(2)}) async-start(), calls=%async_computation.20 | async-start | bytes 5898240 | tf_op jit(solution)/shard_map/reduce_scatter | solution.py:296
  149.4 115.7 %reduce-scatter.17.cloned.1.call-start = ((), (), s32[]{:S(2)}) async-start(), calls=%async_computation.15 | async-start | bytes 1474560 | tf_op jit(solution)/shard_map/reduce_scatter | solution.py:290
  177.7 98.9 %reduce-scatter.21.cloned.1.call-start = ((), (), s32[]{:S(2)}) async-start(), calls=%async_computation.17 | async-start | bytes 5898240 | tf_op jit(solution)/shard_map/reduce_scatter | solution.py:293
  188.3 131.3 %reduce-scatter.13.cloned.1.call-start = ((), (), s32[]{:S(2)}) async-start(), calls=%async_computation.13 | async-start | bytes 4423680 | tf_op jit(solution)/shard_map/reduce_scatter | solution.py:287
  243.1 99.4 %reduce-scatter.29.cloned.1.call-start = ((), (), s32[]{:S(2)}) async-start(), calls=%async_computation.22 | async-start | bytes 245760
  262.1 154.6 %reduce-scatter.27.cloned.1.call-start = ((), (), s32[]{:S(2)}) async-start(), calls=%async_computation.21 | async-start | bytes 2654208 | tf_op jit(solution)/shard_map/reduce_scatter | solution.py:307
  265.0 217.6 %reduce-scatter.19.cloned.1.call-start = ((), (), s32[]{:S(2)}) async-start(), calls=%async_computation.16 | async-start | bytes 663552 | tf_op jit(solution)/shard_map/reduce_scatter | solution.py:305
  266.9 290.5 %reduce-scatter.23.cloned.1.call-start = ((), (), s32[]{:S(2)}) async-start(), calls=%async_computation.18 | async-start | bytes 2654208 | tf_op jit(solution)/shard_map/reduce_scatter | solution.py:306
  279.6 355.1 %reduce-scatter.15.cloned.1.call-start = ((), (), s32[]{:S(2)}) async-start(), calls=%async_computation.14 | async-start | bytes 1990656 | tf_op jit(solution)/shard_map/reduce_scatter | solution.py:304
  322.2 358.6 %all-gather.16.cloned.1.call-start = ((), (), s32[]{:S(2)}) async-start(), calls=%async_computation.19 | async-start | bytes 1327104 | tf_op jit(solution)/shard_map/all_gather | solution.py:329
  322.2 58.8 %copy-start.38 = (f32[14,192]{1,0:T(8,128)S(1)}, f32[14,192]{1,0:T(8,128)}, u32[]{:S(2)}) copy-start(f32[14,192]{1,0:T(8,128)} %param.35) | copy-start | bytes 32260
  322.3 94.4 %copy-start.23 = (f32[96,768]{1,0:T(8,128)S(1)}, f32[96,768]{1,0:T(8,128)}, u32[]{:S(2)}) copy-start(f32[96,768]{1,0:T(8,128)} %param.33) | copy-start | bytes 884740
  322.3 160.3 %copy-start.28 = (f32[24,768]{1,0:T(8,128)S(1)}, f32[24,768]{1,0:T(8,128)}, u32[]{:S(2)}) copy-start(f32[24,768]{1,0:T(8,128)} %param.27) | copy-start | bytes 221188
  331.7 225.7 %copy-start.24 = (f32[24,3072]{1,0:T(8,128)S(1)}, f32[24,3072]{1,0:T(8,128)}, u32[]{:S(2)}) copy-start(f32[24,3072]{1,0:T(8,128)} %param.30) | copy-start | bytes 884740
  331.7 225.7 %copy-start.25 = (f32[24,3072]{1,0:T(8,128)S(1)}, f32[24,3072]{1,0:T(8,128)}, u32[]{:S(2)}) copy-start(f32[24,3072]{1,0:T(8,128)} %param.31) | copy-start | bytes 884740
  418.8 97.9 %collective-permute-start = (bf16[1,96,768]{2,1,0:T(8,128)(2,1)S(1)}, bf16[1,96,768]{2,1,0:T(8,128)(2,1)S(1)}, u32[]{:S(2)}, u32[]{:S(2)}) collective-permute-start(bf16[1,96,768]{2,1,0:T(8,128)(2,1)S(1)} %bitcast.187), channel_id=1, source_target_pairs={{0,4},{4,0},{8,12},{12,8},{16,20},{20,16},{24,28},{28,24},{1,5},{5... | collective-permute-start | bytes 442376 | tf_op jit(solution)/shard_map/ppermute | solution.py:34
  516.7 118.0 %copy-start.26 = (f32[24,2304]{1,0:T(8,128)S(1)}, f32[24,2304]{1,0:T(8,128)}, u32[]{:S(2)}) copy-start(f32[24,2304]{1,0:T(8,128)} %param.24) | copy-start | bytes 663556
  516.7 118.0 %copy-start.27 = (f32[24,2304]{1,0:T(8,128)S(1)}, f32[24,2304]{1,0:T(8,128)}, u32[]{:S(2)}) copy-start(f32[24,2304]{1,0:T(8,128)} %param.25) | copy-start | bytes 663556
  516.8 42.6 %collective-permute-start.1 = (bf16[2,96,768]{2,1,0:T(8,128)(2,1)S(1)}, bf16[2,96,768]{2,1,0:T(8,128)(2,1)S(1)}, u32[]{:S(2)}, u32[]{:S(2)}) collective-permute-start(bf16[2,96,768]{2,1,0:T(8,128)(2,1)S(1)} %get-tuple-element.61), channel_id=1, source_target_pairs={{0,8},{4,12},{8,0},{12,4},{16,24},{20,28},{24,16},{28,20},{1,9},{5... | collective-permute-start | bytes 884744 | tf_op jit(solution)/shard_map/ppermute | solution.py:34
  559.7 112.5 %collective-permute-start.2 = (bf16[4,96,768]{2,1,0:T(8,128)(2,1)S(1)}, bf16[4,96,768]{2,1,0:T(8,128)(2,1)S(1)}, u32[]{:S(2)}, u32[]{:S(2)}) collective-permute-start(bf16[4,96,768]{2,1,0:T(8,128)(2,1)S(1)} %bitcast.182), channel_id=1, source_target_pairs={{0,16},{4,20},{8,24},{12,28},{16,0},{20,4},{24,8},{28,12},{1,17},{... | collective-permute-start | bytes 1769480 | tf_op jit(solution)/shard_map/ppermute | solution.py:34
  (46 other events, 526.6 us)
Sparse Core Ops, SparseCore 0:
  10.2 33.4 all-gather.7
  45.8 17.4 all-gather.9
  65.4 37.4 all-gather.11
  104.3 37.4 all-gather.13
  149.5 47.9 reduce-scatter.24
  200.5 25.6 reduce-scatter.16
  228.7 47.9 reduce-scatter.20
  279.2 40.3 reduce-scatter.12
  322.7 19.7 reduce-scatter.28
  346.4 70.2 reduce-scatter.26
  420.6 61.9 reduce-scatter.18
  486.5 70.8 reduce-scatter.22
  561.4 73.2 reduce-scatter.14
  637.4 43.3 all-gather.15
